TPU v7x, 256 devices: a whole 4x4x8 slice. The times are simulated.
256 devices in a mesh: dp: 4 (over x), expert: 64 (over y, z, core).
Axes of the slice: x: 4, y: 4, z: 8, core: 2. Of those that a mesh axis runs over, the one named last changes fastest.
Arguments:
- tokens: bfloat16 [32768, 2048], P(('dp', 'expert')), may hold values from -6 to 6
- tangent: bfloat16 [32768, 2048], P(('dp', 'expert')), may hold values from -16 to 16
- routes: int32 [32768, 4], P(('dp', 'expert')), may hold values from 0 to 63, all different within a row; in each aligned block of 128 rows (0 to 127, 128 to 255, ...) at most 9 rows name the same one
- gates: float32 [32768, 4], P(('dp', 'expert')), may hold values from 0.05 to 0.5
- w_gate: bfloat16 [64, 2048, 768], P('expert'), may hold values from -0.125 to 0.125
- w_up: bfloat16 [64, 2048, 768], P('expert'), may hold values from -0.125 to 0.125
- w_down: bfloat16 [64, 768, 2048], P('expert'), may hold values from -0.21875 to 0.21875
Outputs:
- product: float32 [32768, 2048], P(('dp', 'expert'))
Inputs may be any that keep to these rules, and one draw needn't show every extreme that they name: `routes`: among the 512 pairs of the rows of one device, no expert is named more than 9 times, a bound that some block reaches.
All inputs are finite; a program needn't handle non-finite values.
Results may differ from a plain program's by a relative error of at most 0.005.
Values may be sent and summed in bfloat16 or wider, within the bound.
A program may use at most 128 MiB of HBM per device.

v0:
```python
import jax
import jax.numpy as jnp
from jax import lax
from jax.sharding import PartitionSpec as P


def owner_states(x_rows, gate_w, up_w):
    pre_a = jnp.dot(x_rows, gate_w, preferred_element_type=jnp.float32)
    pre_b = jnp.dot(x_rows, up_w, preferred_element_type=jnp.float32)
    sigma = jax.nn.sigmoid(pre_a)
    act = pre_a * sigma
    slope = sigma * (1.0 + pre_a * (1.0 - sigma))
    return (pre_b, act, slope)


def shards(tokens, tangent, routes, gates, w_gate, w_up, w_down):
    model_width = tokens.shape[1]
    token_count = tokens.shape[0]
    top_k = routes.shape[1]
    owners = lax.axis_size("expert")
    expert_total = owners * w_gate.shape[0]
    capacity = max(2, token_count * top_k * 9 // (8 * expert_total))
    slot_total = expert_total * capacity
    pair_count = token_count * top_k
    gate_w = w_gate[0]
    up_w = w_up[0]
    down_w = w_down[0]
    flat_routes = routes.reshape(pair_count)
    onehot = (flat_routes[:, None] == jnp.arange(expert_total, dtype=jnp.int32)[None, :]).astype(
        jnp.int32
    )
    before = jnp.cumsum(onehot, axis=0) - onehot
    slot_of = jnp.sum(before * onehot, axis=1)
    slot_index = flat_routes * capacity + slot_of
    slot_match = slot_index[None, :] == jnp.arange(slot_total, dtype=jnp.int32)[:, None]
    filled = jnp.any(slot_match, axis=1)
    pair_token = jnp.arange(pair_count, dtype=jnp.int32) // top_k
    source_token = jnp.sum(jnp.where(slot_match, pair_token[None, :], 0), axis=1)
    source_gate = jnp.sum(
        jnp.where(slot_match, gates.reshape(pair_count)[None, :], jnp.float32(0.0)), axis=1
    )
    keep_mask = filled.astype(jnp.bfloat16)[:, None]
    send_x = (jnp.take(tokens, source_token, axis=0) * keep_mask).reshape(
        owners, capacity, model_width
    )
    send_v = (jnp.take(tangent, source_token, axis=0) * keep_mask).reshape(
        owners, capacity, model_width
    )
    arrived = (
        lax.all_to_all(send_x, "expert", split_axis=0, concat_axis=0, tiled=True),
        lax.all_to_all(send_v, "expert", split_axis=0, concat_axis=0, tiled=True),
    )
    x_rows = arrived[0].reshape(slot_total, model_width)
    v_rows = arrived[1].reshape(slot_total, model_width)
    pre_b, act, slope = owner_states(x_rows, gate_w, up_w)
    tan_a = jnp.dot(v_rows, gate_w, preferred_element_type=jnp.float32)
    tan_b = jnp.dot(v_rows, up_w, preferred_element_type=jnp.float32)
    hidden_tangent = (slope * tan_a * pre_b + act * tan_b).astype(jnp.bfloat16)
    pair_tangent = jnp.dot(hidden_tangent, down_w, preferred_element_type=jnp.float32).astype(
        jnp.bfloat16
    )
    returned = lax.all_to_all(
        pair_tangent.reshape(owners, capacity, model_width),
        "expert",
        split_axis=0,
        concat_axis=0,
        tiled=True,
    )
    picked_rows = jnp.take(returned.reshape(slot_total, model_width), slot_index, axis=0)
    picked_rows = picked_rows.reshape(token_count, top_k, model_width)
    jv_vals = tangent.astype(jnp.float32) + jnp.sum(
        gates[:, :, None] * picked_rows.astype(jnp.float32), axis=1
    )
    cotangent = (jnp.take(jv_vals, source_token, axis=0) * source_gate[:, None]).astype(
        jnp.bfloat16
    )
    cotangent = cotangent.reshape(owners, capacity, model_width)
    cot_rows = lax.all_to_all(cotangent, "expert", split_axis=0, concat_axis=0, tiled=True).reshape(
        slot_total, model_width
    )
    contract_last = (((1,), (1,)), ((), ()))
    back_vals = lax.dot_general(cot_rows, down_w, contract_last, preferred_element_type=jnp.float32)
    grad_gate = (back_vals * pre_b * slope).astype(jnp.bfloat16)
    grad_up = (back_vals * act).astype(jnp.bfloat16)
    pair_grad = (
        lax.dot_general(grad_gate, gate_w, contract_last, preferred_element_type=jnp.float32)
        + lax.dot_general(grad_up, up_w, contract_last, preferred_element_type=jnp.float32)
    ).astype(jnp.bfloat16)
    grads_home = lax.all_to_all(
        pair_grad.reshape(owners, capacity, model_width),
        "expert",
        split_axis=0,
        concat_axis=0,
        tiled=True,
    )
    grad_rows = jnp.take(grads_home.reshape(slot_total, model_width), slot_index, axis=0)
    grad_rows = grad_rows.reshape(token_count, top_k, model_width)
    summed = jv_vals + jnp.sum(grad_rows.astype(jnp.float32), axis=1)
    local_sum = jnp.sum(jv_vals * jv_vals)
    global_sum = lax.psum(local_sum, ("dp", "expert"))
    element_count = token_count * lax.axis_size("dp") * owners * model_width
    return summed * lax.rsqrt(global_sum / element_count + 1e-06)


def solution(mesh):
    placed = (
        P(("dp", "expert"), None),
        P(("dp", "expert"), None),
        P(("dp", "expert"), None),
        P(("dp", "expert"), None),
        P("expert", None, None),
        P("expert", None, None),
        P("expert", None, None),
    )
    return jax.shard_map(
        shards, mesh=mesh, in_specs=placed, out_specs=P(("dp", "expert"), None), check_vma=False
    )
```

profile of v0, /device:TPU:1, one launch (start us, length us, event | category | flops | bytes accessed | tf_op | source)
XLA Modules:
  0.0 709.1 jit_solution(15984406415920495987)
XLA Ops:
  0.0 0.9 copy.15
  1.2 1.2 reduce-window.6
  2.4 0.2 slice_reduce_fusion
  2.8 0.2 fusion.24
  3.0 0.2 select_reduce_fusion.1
  3.3 7.9 %gather_fusion.2 = bf16[576,2048]{1,0:T(8,128)(2,1)} fusion(bf16[128,2048]{1,0:T(8,128)(2,1)} %param.12, s32[1024]{0:T(1024)S(1)} %pad_clamp_fusion.2), kind=kCustom, calls=%fused_computation.2.clone | custom fusion | bytes 4720896 | tf_op jit(solution)/shard_map/jit(_take)/gather | solution.py:46
  11.2 8.0 %gather_fusion.1 = bf16[576,2048]{1,0:T(8,128)(2,1)} fusion(bf16[128,2048]{1,0:T(8,128)(2,1)} %param.11, s32[1024]{0:T(1024)S(1)} %pad_clamp_fusion.2), kind=kCustom, calls=%fused_computation.clone | custom fusion | bytes 4720896 | tf_op jit(solution)/shard_map/jit(_take)/gather | solution.py:43
  19.2 4.3 select_multiply_fusion.1
  23.5 4.6 reshape.122
  28.1 13.3 %all-to-all-start = ((bf16[64,9,2048]{2,1,0:T(8,128)(2,1)}), bf16[64,9,2048]{2,1,0:T(8,128)(2,1)}, u32[]{:S(2)}, u32[]{:S(2)}) async-start(bf16[64,9,2048]{2,1,0:T(8,128)(2,1)} %reshape.122), calls=%async_computation | async-start | bytes 8388608 | tf_op jit(solution)/shard_map/all_to_all | solution.py:50
  41.4 4.6 reshape.124
  46.0 91.2 %all-to-all-done = bf16[64,9,2048]{2,1,0:T(8,128)(2,1)} async-done(((bf16[64,9,2048]{2,1,0:T(8,128)(2,1)}), bf16[64,9,2048]{2,1,0:T(8,128)(2,1)}, u32[]{:S(2)}, u32[]{:S(2)}) %all-to-all-start) | async-done | bytes 2359328 | tf_op jit(solution)/shard_map/all_to_all | solution.py:50
  137.3 6.6 all-to-all-start.1
  143.9 4.7 reshape.123
  148.6 5.0 fusion.14
  153.7 3.2 fusion.8
  156.9 82.7 %all-to-all-done.1 = bf16[64,9,2048]{2,1,0:T(8,128)(2,1)} async-done(((bf16[64,9,2048]{2,1,0:T(8,128)(2,1)}), bf16[64,9,2048]{2,1,0:T(8,128)(2,1)}, u32[]{:S(2)}, u32[]{:S(2)}) %all-to-all-start.1) | async-done | bytes 2359328 | tf_op jit(solution)/shard_map/all_to_all | solution.py:51
  239.6 4.7 reshape.125
  244.3 5.8 fusion.6
  250.0 10.2 %fusion.16 = bf16[576,2048]{1,0:T(8,128)(2,1)} fusion(bf16[1,768,2048]{2,1,0:T(8,128)(2,1)} %param.17, f32[576,768]{1,0:T(8,128)} %fusion.6, f32[576,768]{1,0:T(8,128)} %fusion.8, bf16[576,2048]{1,0:T(8,128)(2,1)} %reshape.125, bf16[1,2048,768]{2,1,0:T(8,128)(2,1)S(1)} %copy-done, f32[576,768]{1,0:T(8,128)} %fusion.14), kind=kOutput, calls=%fused_computation.24 | convolution fusion | flops 3630809088 | bytes 16318464 | tf_op jit(solution)/shard_map/dot_general | solution.py:59
  260.2 4.6 reshape.126
  264.8 6.5 all-to-all-start.2
  271.7 0.2 select_reduce_fusion
  271.9 0.1 mul.96
  272.1 94.9 %all-to-all-done.2 = bf16[64,9,2048]{2,1,0:T(8,128)(2,1)} async-done(((bf16[64,9,2048]{2,1,0:T(8,128)(2,1)}), bf16[64,9,2048]{2,1,0:T(8,128)(2,1)}, u32[]{:S(2)}, u32[]{:S(2)}) %all-to-all-start.2) | async-done | bytes 2359328 | tf_op jit(solution)/shard_map/all_to_all | solution.py:62
  367.0 4.7 reshape.127
  371.6 7.2 %gather_fusion.3 = bf16[512,2048]{1,0:T(8,128)(2,1)} fusion(bf16[576,2048]{1,0:T(8,128)(2,1)} %reshape.127, s32[1024]{0:T(1024)S(1)} %pad_clamp_fusion.1), kind=kCustom, calls=%fused_computation.1.clone | custom fusion | bytes 4196352 | tf_op jit(solution)/shard_map/jit(_take)/gather | solution.py:69
  378.9 3.9 select_convert_fusion.1
  382.7 5.2 reshape.131
  387.9 5.5 multiply_reduce_fusion
  393.4 1.9 multiply_reduce_fusion.1
  395.2 7.9 %gather_fusion = f32[576,2048]{1,0:T(8,128)} fusion(f32[128,2048]{1,0:T(8,128)} %get-tuple-element.8, s32[1024]{0:T(1024)S(1)} %pad_clamp_fusion), kind=kCustom, calls=%fused_computation.4 | custom fusion | bytes 9439488 | tf_op jit(solution)/shard_map/jit(_take)/gather | solution.py:74
  403.2 6.2 gather.13
  409.4 3.9 multiply_convert_fusion
  413.3 102.1 %all_to_all.25 = bf16[64,9,2048]{2,1,0:T(8,128)(2,1)} all-to-all(bf16[64,9,2048]{2,1,0:T(8,128)(2,1)S(1)} %multiply_convert_fusion), channel_id=1, replica_groups=mesh['dp'=4,'expert'=64] {'expert'}, dimensions={0} | all-to-all | bytes 4718592 | tf_op jit(solution)/shard_map/all_to_all | solution.py:78
  515.5 4.7 reshape.128
  520.1 4.8 fusion
  524.9 2.1 fusion.4
  527.0 3.8 add_convert_fusion
  530.8 4.6 reshape.129
  535.4 6.0 all-to-all-start.4
  541.4 137.4 %psum.7 = f32[]{:T(128)} all-reduce(f32[]{:T(128)} %get-tuple-element.6), channel_id=1, replica_groups=mesh['dp'=4,'expert'=64] {'dp','expert'}, use_global_device_ids=true, to_apply=%region_9.12 | all-reduce | flops 1 | bytes 8 | tf_op jit(solution)/shard_map/psum | solution.py:100
  679.4 4.7 reshape.130
  684.1 7.2 %gather_fusion.4 = bf16[512,2048]{1,0:T(8,128)(2,1)} fusion(bf16[576,2048]{1,0:T(8,128)(2,1)} %reshape.130, s32[1024]{0:T(1024)S(1)} %pad_clamp_fusion.1), kind=kCustom, calls=%fused_computation.3.clone | custom fusion | bytes 4196352 | tf_op jit(solution)/shard_map/jit(_take)/gather | solution.py:96
  691.4 3.9 select_convert_fusion
  695.2 5.2 reshape.132
  700.4 5.8 reduce_sum.64
  706.2 2.6 add_multiply_fusion.1
  (37 shorter events, 0.9 us)
Async XLA Ops:
  0.0 148.6 %copy-start = (bf16[1,2048,768]{2,1,0:T(8,128)(2,1)S(1)}, bf16[1,2048,768]{2,1,0:T(8,128)(2,1)}, u32[]{:S(2)}) copy-start(bf16[1,2048,768]{2,1,0:T(8,128)(2,1)} %param.15) | copy-start | bytes 9437188
  28.1 109.2 %all-to-all-start = ((bf16[64,9,2048]{2,1,0:T(8,128)(2,1)}), bf16[64,9,2048]{2,1,0:T(8,128)(2,1)}, u32[]{:S(2)}, u32[]{:S(2)}) async-start(bf16[64,9,2048]{2,1,0:T(8,128)(2,1)} %reshape.122), calls=%async_computation | async-start | bytes 8388608 | tf_op jit(solution)/shard_map/all_to_all | solution.py:50
  137.3 102.3 %all-to-all-start.1 = ((bf16[64,9,2048]{2,1,0:T(8,128)(2,1)}), bf16[64,9,2048]{2,1,0:T(8,128)(2,1)}, u32[]{:S(2)}, u32[]{:S(2)}) async-start(bf16[64,9,2048]{2,1,0:T(8,128)(2,1)} %reshape.124), calls=%async_computation.1 | async-start | bytes 8388608 | tf_op jit(solution)/shard_map/all_to_all | solution.py:51
  148.6 5.0 copy-start.2
  148.6 5.0 copy-start.4
  264.8 6.6 copy-start.3
  264.8 102.1 %all-to-all-start.2 = ((bf16[64,9,2048]{2,1,0:T(8,128)(2,1)}), bf16[64,9,2048]{2,1,0:T(8,128)(2,1)}, u32[]{:S(2)}, u32[]{:S(2)}) async-start(bf16[64,9,2048]{2,1,0:T(8,128)(2,1)} %reshape.126), calls=%async_computation.2 | async-start | bytes 8388608 | tf_op jit(solution)/shard_map/all_to_all | solution.py:62
  387.9 5.5 copy-start.1
  520.1 4.8 copy-start.5
  520.1 4.8 copy-start.6
  524.9 2.1 copy-start.7
  535.4 144.0 %all-to-all-start.4 = ((bf16[64,9,2048]{2,1,0:T(8,128)(2,1)}), bf16[64,9,2048]{2,1,0:T(8,128)(2,1)}, u32[]{:S(2)}, u32[]{:S(2)}) async-start(bf16[64,9,2048]{2,1,0:T(8,128)(2,1)} %reshape.129), calls=%async_computation.4 | async-start | bytes 8388608 | tf_op jit(solution)/shard_map/all_to_all | solution.py:89
where the time goes:
time: 717 us; the launch traced here: 709 us
  waiting for transfers between devices  269 us (38%)
  blocking collectives  240 us (33%)
  local copies, waits for them, and re-layouts  98.5 us (14%)
  matrix products  34.9 us (5%)
  other arithmetic  33.9 us (5%)
  starting transfers between devices  32.4 us (5%)
    psum x1, blocking collectives, shards(): global_sum = lax.psum(local_sum, ('dp', 'expert'))  137 us
    all_to_all x1, blocking collectives, shards(): lax.all_to_all(cotangent, 'expert', split_axis=0, concat_axis=0, tiled=True)  102 us
    all_to_all x1, waiting for transfers between devices, shards(): lax.all_to_all(pair_tangent.reshape(owners, capacity, model_width), 'expe...  94.9 us
    all_to_all x1, waiting for transfers between devices, shards(): lax.all_to_all(send_x, 'expert', split_axis=0, concat_axis=0, tiled=True)  91.2 us
    all_to_all x1, waiting for transfers between devices, shards(): lax.all_to_all(send_v, 'expert', split_axis=0, concat_axis=0, tiled=True)  82.7 us
  transfers between devices with their start and end apart: 4, of which 3 were waited for; matrix products, arithmetic and copies ran while one was open for 3% of the time, Pallas kernels for 0%

commit v1 on v0

v1 whole, which is shorter than its diff:
```python
import functools
import jax
import jax.numpy as jnp
from jax import lax
from jax.experimental import pallas as pl
from jax.experimental.pallas import tpu as pltpu
from jax.sharding import PartitionSpec as P

MESH = pl.DeviceIdType.MESH
F32 = jnp.float32
BF16 = jnp.bfloat16
CAP = 9
STG = 3


def body(
    ny, nz, nx, dims, x_hbm, v_hbm, rt_ref, gt_ref, wg_hbm, wu_hbm, wd_hbm, out_hbm,
    wg, wu, wd, g, r, sel, selt, acc, hid, gru, ret, yb, rs, stg, rstg, jvf, ostg,
    metas, metar, gsend, grecv, red, ssacc,
    load_sem, w_sem, ag_r, ag_s, y_r, y_s, rt_r, rt_s, rs_r, rs_s, o_sem, meta_sem, gate_sem, red_sem,
):
    tok, width, rows, nch, ff = dims
    peers = 2 * ny
    half = nz // 2
    total = peers * rows
    me = lax.axis_index("expert")
    mx = lax.axis_index("dp")
    my = me // (2 * nz)
    mz = lax.rem(me // 2, nz)
    mc = lax.rem(me, 2)
    mp = my * 2 + mc

    def zdev(zt):
        return my * (2 * nz) + zt * 2 + mc

    def pdev(d):
        return (d // 2) * (2 * nz) + mz * 2 + lax.rem(d, 2)

    def zoff(k):
        return lax.rem(mz + (k + nz), nz)

    right = zdev(zoff(1))
    left = zdev(zoff(-1))

    def local(src, dst, sem):
        return pltpu.make_async_copy(src, dst, sem)

    def remote(src, dst, ssem, rsem, dev):
        return pltpu.make_async_remote_copy(
            src_ref=src, dst_ref=dst, send_sem=ssem, recv_sem=rsem,
            device_id={"expert": dev}, device_id_type=MESH,
        )

    def load(i, hbm, ch):
        return local(hbm.at[:, pl.ds(ch * width, width)], g.at[i, mz], load_sem.at[i])

    for ch in range(nch):
        load(2 * ch, x_hbm, ch).start()
        load(2 * ch + 1, v_hbm, ch).start()
    for ch in range(nch):
        local(wg_hbm.at[0, pl.ds(ch * width, width), :], wg.at[ch], w_sem.at[0]).start()
        local(wu_hbm.at[0, pl.ds(ch * width, width), :], wu.at[ch], w_sem.at[1]).start()
    for ch in range(nch):
        local(wd_hbm.at[0, :, pl.ds(ch * width, width)], wd.at[ch], w_sem.at[2]).start()

    barrier = pltpu.get_barrier_semaphore()
    for k in range(1, nz):
        pl.semaphore_signal(barrier, inc=1, device_id={"expert": zdev(zoff(k))}, device_id_type=MESH)
    for k in range(1, peers):
        pl.semaphore_signal(
            barrier, inc=1, device_id={"expert": pdev(lax.rem(mp + k, peers))}, device_id_type=MESH
        )
    for k in range(1, nx):
        pl.semaphore_signal(
            barrier, inc=1, device_id={"dp": lax.rem(mx + k, nx)}, device_id_type=MESH
        )

    pshift = peers.bit_length() - 1
    row = lax.broadcasted_iota(jnp.int32, (nz * peers, tok), 0)
    zrow = lax.shift_right_logical(row, pshift)
    drow = jnp.bitwise_and(row, peers - 1)
    expert = lax.shift_right_logical(drow, 1) * (2 * nz) + zrow * 2 + jnp.bitwise_and(drow, 1)
    named = jnp.zeros((nz * peers, tok), F32)
    weight = jnp.zeros((nz * peers, tok), F32)
    for k in range(rt_ref.shape[0]):
        hit = jnp.broadcast_to(rt_ref[k : k + 1, :], expert.shape) == expert
        named = named + jnp.where(hit, 1.0, 0.0)
        weight = weight + jnp.where(hit, jnp.broadcast_to(gt_ref[k : k + 1, :], expert.shape), 0.0)
    earlier = lax.broadcasted_iota(jnp.int32, (tok, tok), 0) < lax.broadcasted_iota(
        jnp.int32, (tok, tok), 1
    )
    rank = jnp.dot(
        named.astype(BF16), jnp.where(earlier, 1.0, 0.0).astype(BF16), preferred_element_type=F32
    )
    base = (mz * CAP).astype(F32)
    code = jnp.where(named > 0.5, rank + base, -1.0)
    for zt in range(nz):
        metas[zt, 0:peers, :] = code[zt * peers : (zt + 1) * peers]
        metas[zt, peers : 2 * peers, :] = weight[zt * peers : (zt + 1) * peers]
    metar[mz] = metas[mz]

    @pl.loop(0, total // 16)
    def _(q):
        for m in range(4):
            acc[m, pl.ds(pl.multiple_of(q * 16, 16), 16), :] = jnp.zeros((16, ff), F32)

    ssacc[...] = jnp.zeros(ssacc.shape, F32)
    pl.semaphore_wait(barrier, (nz - 1) + (peers - 1) + (nx - 1))

    for k in range(1, nz):
        zt = zoff(k)
        remote(metas.at[zt], metar.at[mz], meta_sem.at[0], meta_sem.at[1], zdev(zt)).start()

    def ag_send(i, slot, zs, dev):
        remote(g.at[i, zs], g.at[i, zs], ag_s.at[i], ag_r.at[i, slot], dev).start()

    def ag_wait(i, slot):
        remote(g.at[i, mz], g.at[i, mz], ag_s.at[i], ag_r.at[i, slot], right).wait_recv()

    def ag_first(i):
        ag_send(i, 0, mz, right)
        ag_send(i, 1, mz, left)

    def ag_mid(i, s):
        ag_wait(i, 2 * (s - 2))
        ag_send(i, 2 * (s - 1), zoff(-(s - 1)), right)
        ag_wait(i, 2 * (s - 2) + 1)
        ag_send(i, 2 * (s - 1) + 1, zoff(s - 1), left)

    def ag_far(i, par):
        ag_wait(i, 2 * (half - 2))
        ag_wait(i, 2 * (half - 2) + 1)
        zs = jnp.where(par == 0, zoff(-(half - 1)), zoff(half - 1))
        ag_send(i, 2 * half - 2, zs, jnp.where(par == 0, right, left))

    def ag_done(i):
        ag_wait(i, 2 * half - 2)

    def ag_drain(i):
        local(g.at[i, pl.ds(0, nz - 1)], g.at[i, pl.ds(0, nz - 1)], ag_s.at[i]).wait()

    def dispatch(i, slot):
        tokens = g[i].reshape(nz * tok, width)
        for d in range(peers):
            stg[slot, d] = jnp.dot(
                sel[d * rows : (d + 1) * rows, :], tokens, preferred_element_type=F32
            ).astype(BF16)

    def dispatch_send(i, slot):
        for k in range(1, peers):
            d = lax.rem(mp + k, peers)
            remote(stg.at[slot, d], r.at[i, mp], y_s.at[slot], y_r.at[i], pdev(d)).start()
        local(stg.at[slot, mp], r.at[i, mp], y_r.at[i]).start()

    def dispatch_wait(i, slot):
        local(r.at[i], r.at[i], y_r.at[i]).wait()
        local(
            stg.at[slot, pl.ds(0, peers - 1)], stg.at[slot, pl.ds(0, peers - 1)], y_s.at[slot]
        ).wait()

    def return_send(j, slot):
        for k in range(1, peers):
            d = lax.rem(mp + k, peers)
            remote(rstg.at[slot, d], ret.at[j, mp], rt_s.at[slot], rt_r.at[j], pdev(d)).start()
        local(rstg.at[slot, mp], ret.at[j, mp], rt_r.at[j]).start()

    def combine(j, slot):
        local(ret.at[j], ret.at[j], rt_r.at[j]).wait()
        local(
            rstg.at[slot, pl.ds(0, peers - 1)], rstg.at[slot, pl.ds(0, peers - 1)], rt_s.at[slot]
        ).wait()
        back_rows = ret[j].reshape(total, width)
        for zs in range(nz):
            yb[j, zs] = jnp.dot(
                selt[zs * tok : (zs + 1) * tok, :], back_rows, preferred_element_type=F32
            ).astype(BF16)

    far = 2 * (half - 1)

    def rs_send(j, src, slot, dev):
        remote(src, rs.at[j, slot], rs_s.at[j], rs_r.at[j, slot], dev).start()

    def rs_wait(j, slot):
        remote(rs.at[j, slot], rs.at[j, slot], rs_s.at[j], rs_r.at[j, slot], right).wait_recv()

    def rs_add(j, slot, zd):
        rs[j, slot] = (rs[j, slot].astype(F32) + yb[j, zd].astype(F32)).astype(BF16)

    def rs_first(j, par):
        rs_send(j, yb.at[j, zoff(half)], far, jnp.where(par == 0, right, left))
        zd = jnp.where(par == 0, zoff(-(half - 1)), zoff(half - 1))
        rs_send(j, yb.at[j, zd], 1 - par, jnp.where(par == 0, left, right))

    def rs_second(j, par):
        rs_wait(j, far)
        rs_add(j, far, jnp.where(par == 0, zoff(half - 1), zoff(-(half - 1))))
        rs_send(j, rs.at[j, far], par, jnp.where(par == 0, right, left))

    def rs_mid(j, s):
        rs_wait(j, 2 * (s - 2))
        rs_add(j, 2 * (s - 2), zoff(half - s))
        rs_wait(j, 2 * (s - 2) + 1)
        rs_add(j, 2 * (s - 2) + 1, zoff(-(half - s)))
        rs_send(j, rs.at[j, 2 * (s - 2)], 2 * (s - 1), right)
        rs_send(j, rs.at[j, 2 * (s - 2) + 1], 2 * (s - 1) + 1, left)

    def rs_final(j):
        rs_wait(j, far - 2)
        rs_wait(j, far - 1)
        return (
            rs[j, far - 2].astype(F32) + rs[j, far - 1].astype(F32) + yb[j, mz].astype(F32)
        )

    def rs_drain(j):
        local(rs.at[j], rs.at[j], rs_s.at[j]).wait()

    def at(lag, count, tick, fn):
        i = tick - lag

        @pl.when((i >= 0) & (i < count))
        def _():
            fn(i)

    nitem = 2 * nch

    def first(i):
        load(i, x_hbm, 0).wait()
        ag_first(i)

    def products(i):
        dispatch_wait(i, lax.rem(i, STG))
        ch = i // 2
        m = lax.rem(i, 2) * 2
        got = r[i].reshape(total, width)
        for n in range(ff // width):
            cols = slice(n * width, (n + 1) * width)
            acc[m, :, cols] += jnp.dot(got, wg[ch, :, cols], preferred_element_type=F32)
            acc[m + 1, :, cols] += jnp.dot(got, wu[ch, :, cols], preferred_element_type=F32)

    def spread(i):
        ag_done(i)
        dispatch(i, lax.rem(i, STG))
        dispatch_send(i, lax.rem(i, STG))

    def build():
        local(metar.at[pl.ds(0, nz - 1)], metar.at[pl.ds(0, nz - 1)], meta_sem.at[1]).wait()
        local(metas.at[pl.ds(0, nz - 1)], metas.at[pl.ds(0, nz - 1)], meta_sem.at[0]).wait()
        slot_id = lax.broadcasted_iota(jnp.int32, (peers, rows, tok), 1).astype(F32)
        slot_id = slot_id.reshape(total, tok)
        gates = jnp.zeros((total, tok), F32)
        for zs in range(nz):
            q = jnp.broadcast_to(metar[zs, 0:peers, :][:, None, :], (peers, rows, tok))
            w = jnp.broadcast_to(metar[zs, peers : 2 * peers, :][:, None, :], (peers, rows, tok))
            same = q.reshape(total, tok) == slot_id
            one = jnp.where(same, 1.0, 0.0)
            sel[:, zs * tok : (zs + 1) * tok] = one.astype(BF16)
            selt[zs * tok : (zs + 1) * tok, :] = one.T.astype(BF16)
            gates = gates + jnp.where(same, w.reshape(total, tok), 0.0)
        gate = jnp.broadcast_to(jnp.sum(gates, axis=1, keepdims=True), (total, tok))
        gsend[...] = gate.reshape(peers, rows, tok)
        for k in range(1, peers):
            d = lax.rem(mp + k, peers)
            remote(gsend.at[d], grecv.at[mp], gate_sem.at[0], gate_sem.at[1], pdev(d)).start()
        local(gsend.at[mp], grecv.at[mp], gate_sem.at[1]).start()

    def tick_a(t, carry):
        at(half - 1, nitem, t, lambda i: ag_far(i, lax.rem(i, 2)))
        for s in range(half - 1, 1, -1):
            at(s - 1, nitem, t, lambda i, s=s: ag_mid(i, s))
        at(0, nitem, t, first)

        @pl.when(t == half - 1)
        def _():
            build()

        at(half, nitem, t, spread)

        @pl.when(t == half + 1)
        def _():
            for q, (hbm, vm) in enumerate(((wg_hbm, wg), (wu_hbm, wu), (wd_hbm, wd))):
                local(vm, vm, w_sem.at[q]).wait()

        at(half + 2, nitem, t, products)
        at(half + 2, nitem, t, ag_drain)
        return carry

    lax.fori_loop(0, nitem + half + 2, tick_a, 0)

    local(grecv, grecv, gate_sem.at[1]).wait()
    local(gsend.at[pl.ds(0, peers - 1)], gsend.at[pl.ds(0, peers - 1)], gate_sem.at[0]).wait()

    @pl.loop(0, total // 16)
    def _(q):
        at_rows = pl.ds(pl.multiple_of(q * 16, 16), 16)
        a = acc[0, at_rows, :]
        b = acc[1, at_rows, :]
        s = jax.nn.sigmoid(a)
        act = a * s
        slope_b = s * (1.0 + a * (1.0 - s)) * b
        hid[at_rows, :] = (slope_b * acc[2, at_rows, :] + act * acc[3, at_rows, :]).astype(BF16)
        acc[0, at_rows, :] = act
        acc[1, at_rows, :] = slope_b
        acc[2, at_rows, :] = jnp.zeros((16, ff), F32)

    def gate_lanes():
        gl = grecv[...].reshape(total, tok)
        return jnp.concatenate([gl] * (width // tok), axis=1)

    def tangent_out(j):
        slot = lax.rem(j, STG)
        pt = jnp.dot(hid[...], wd[j], preferred_element_type=F32) * gate_lanes()
        rstg[slot] = pt.astype(BF16).reshape(peers, rows, width)
        return_send(j, slot)

    def home(j):
        combine(j, lax.rem(j, STG))
        rs_first(j, lax.rem(j, 2))

    def finish_jv(j):
        jv = rs_final(j) + g[2 * j + 1, mz].astype(F32)
        jvf[j] = jv
        ssacc[...] += jv * jv
        g[2 * j, mz] = jv.astype(BF16)
        ag_first(2 * j)

    def spread_jv(j):
        rs_drain(j)
        ag_done(2 * j)
        dispatch(2 * j, lax.rem(j, STG))
        dispatch_send(2 * j, lax.rem(j, STG))

    contract_last = (((1,), (1,)), ((), ()))

    def back(j):
        dispatch_wait(2 * j, lax.rem(j, STG))
        ag_drain(2 * j)
        got = r[2 * j].reshape(total, width)
        for n in range(ff // width):
            cols = slice(n * width, (n + 1) * width)
            acc[2, :, cols] += lax.dot_general(
                got, wd[j, cols, :], contract_last, preferred_element_type=F32
            )

    rl = 2
    al = rl + half

    def tick_b(t, carry):
        at(al + half - 1, nch, t, lambda j: ag_far(2 * j, lax.rem(j, 2)))
        for s in range(half - 1, 1, -1):
            at(al + s - 1, nch, t, lambda j, s=s: ag_mid(2 * j, s))
        for s in range(half - 1, 1, -1):
            at(rl + s, nch, t, lambda j, s=s: rs_mid(j, s))
        at(rl + 1, nch, t, lambda j: rs_second(j, lax.rem(j, 2)))
        at(al, nch, t, finish_jv)
        at(0, nch, t, tangent_out)
        at(al + half, nch, t, spread_jv)
        at(rl, nch, t, home)
        at(al + half + 2, nch, t, back)
        return carry

    lax.fori_loop(0, nch + al + half + 2, tick_b, 0)

    def exchange(stage, me_slot, count, dev_of):
        for k in range(1, count):
            d = lax.rem(me_slot + k, count)
            pltpu.make_async_remote_copy(
                src_ref=red.at[stage, me_slot], dst_ref=red.at[stage, me_slot],
                send_sem=red_sem.at[0, stage], recv_sem=red_sem.at[1, stage],
                device_id=dev_of(d), device_id_type=MESH,
            ).start()

    def gathered(stage, count):
        span = red.at[stage, pl.ds(0, count - 1)]
        local(span, span, red_sem.at[1, stage]).wait()
        local(span, span, red_sem.at[0, stage]).wait()
        value = red[stage, 0]
        for k in range(1, count):
            value = value + red[stage, k]
        return value

    part = jnp.sum(jnp.sum(ssacc[...], axis=1, keepdims=True), axis=0, keepdims=True)
    red[0, mp] = jnp.broadcast_to(part, (8, 128))
    if peers > 1:
        exchange(0, mp, peers, lambda d: {"expert": pdev(d)})

    @pl.loop(0, total // 16)
    def _(q):
        at_rows = pl.ds(pl.multiple_of(q * 16, 16), 16)
        gl = grecv[q // (rows // 16), pl.ds(pl.multiple_of(lax.rem(q, rows // 16) * 16, 16), 16), :]
        bk = acc[2, at_rows, :] * jnp.concatenate([gl] * (ff // tok), axis=1)
        gru[0, at_rows, :] = (bk * acc[1, at_rows, :]).astype(BF16)
        gru[1, at_rows, :] = (bk * acc[0, at_rows, :]).astype(BF16)

    red[1, mz] = gathered(0, peers)
    exchange(1, mz, nz, lambda d: {"expert": zdev(d)})

    def grad_out(j):
        slot = lax.rem(j, STG)
        pg = lax.dot_general(gru[0], wg[j], contract_last, preferred_element_type=F32)
        pg = pg + lax.dot_general(gru[1], wu[j], contract_last, preferred_element_type=F32)
        rstg[slot] = pg.astype(BF16).reshape(peers, rows, width)
        return_send(j, slot)

    def out_copy(j, slot):
        return local(ostg.at[slot], out_hbm.at[:, pl.ds(pl.multiple_of(j * width, width), width)], o_sem.at[slot])

    def finish_out(j):
        slot = lax.rem(j, 2)

        @pl.when(j >= 2)
        def _():
            out_copy(j - 2, slot).wait()

        mean = red[3, 0][0:1, 0:1] * (1.0 / (tok * nx * ny * nz * 2.0 * nch * width))
        scale = jnp.broadcast_to(lax.rsqrt(mean + 1e-06), (tok, width))
        ostg[slot] = (rs_final(j) + jvf[j]) * scale
        out_copy(j, slot).start()

    def tick_d(t, carry):
        for s in range(half - 1, 1, -1):
            at(rl + s, nch, t, lambda j, s=s: rs_mid(j, s))
        at(rl + 1, nch, t, lambda j: rs_second(j, lax.rem(j, 2)))
        at(0, nch, t, grad_out)
        at(rl, nch, t, home)

        @pl.when(t == rl + 1)
        def _():
            red[2, mx] = gathered(1, nz)
            if nx > 1:
                exchange(2, mx, nx, lambda d: {"dp": d})

        @pl.when(t == al)
        def _():
            red[3, 0] = gathered(2, nx) if nx > 1 else red[2, 0]

        at(al, nch, t, finish_out)
        return carry

    lax.fori_loop(0, nch + al, tick_d, 0)
    for j in range(nch):
        rs_drain(j)
    for j in range(max(0, nch - 2), nch):
        out_copy(j, j % 2).wait()


def shards(ny, nz, nx, tokens, tangent, routes, gates, w_gate, w_up, w_down):
    tok, depth = tokens.shape
    ff = w_gate.shape[2]
    width = 256
    nch = depth // width
    peers = 2 * ny
    rows = -(-(nz * CAP) // 16) * 16
    total = peers * rows
    slots = max(nz, peers, nx)
    dma = pltpu.SemaphoreType.DMA
    scratch = [
        pltpu.VMEM((nch, width, ff), BF16),
        pltpu.VMEM((nch, width, ff), BF16),
        pltpu.VMEM((nch, ff, width), BF16),
        pltpu.VMEM((2 * nch, nz, tok, width), BF16),
        pltpu.VMEM((2 * nch, peers, rows, width), BF16),
        pltpu.VMEM((total, nz * tok), BF16),
        pltpu.VMEM((nz * tok, total), BF16),
        pltpu.VMEM((4, total, ff), F32),
        pltpu.VMEM((total, ff), BF16),
        pltpu.VMEM((2, total, ff), BF16),
        pltpu.VMEM((nch, peers, rows, width), BF16),
        pltpu.VMEM((nch, nz, tok, width), BF16),
        pltpu.VMEM((nch, nz - 1, tok, width), BF16),
        pltpu.VMEM((STG, peers, rows, width), BF16),
        pltpu.VMEM((STG, peers, rows, width), BF16),
        pltpu.VMEM((nch, tok, width), F32),
        pltpu.VMEM((2, tok, width), F32),
        pltpu.VMEM((nz, 2 * peers, tok), F32),
        pltpu.VMEM((nz, 2 * peers, tok), F32),
        pltpu.VMEM((peers, rows, tok), F32),
        pltpu.VMEM((peers, rows, tok), F32),
        pltpu.VMEM((4, slots, 8, 128), F32),
        pltpu.VMEM((tok, width), F32),
        dma((2 * nch,)),
        dma((3,)),
        dma((2 * nch, nz - 1)),
        dma((2 * nch,)),
        dma((2 * nch,)),
        dma((STG,)),
        dma((nch,)),
        dma((STG,)),
        dma((nch, nz - 1)),
        dma((nch,)),
        dma((2,)),
        dma((2,)),
        dma((2,)),
        dma((2, 3)),
    ]
    anywhere = pl.BlockSpec(memory_space=pl.ANY)
    vmem = pl.BlockSpec(memory_space=pltpu.VMEM)
    return pl.pallas_call(
        functools.partial(body, ny, nz, nx, (tok, width, rows, nch, ff)),
        out_shape=jax.ShapeDtypeStruct((tok, depth), F32),
        in_specs=[anywhere, anywhere, vmem, vmem, anywhere, anywhere, anywhere],
        out_specs=anywhere,
        scratch_shapes=scratch,
        compiler_params=pltpu.CompilerParams(
            collective_id=0, has_side_effects=True, vmem_limit_bytes=67043328
        ),
        name="gauss_newton_moe",
    )(tokens, tangent, routes.T, gates.T, w_gate, w_up, w_down)


def build(mesh, ny, nz):
    placed = (
        P(("dp", "expert"), None),
        P(("dp", "expert"), None),
        P(("dp", "expert"), None),
        P(("dp", "expert"), None),
        P("expert", None, None),
        P("expert", None, None),
        P("expert", None, None),
    )
    return jax.shard_map(
        functools.partial(shards, ny, nz, mesh.shape["dp"]),
        mesh=mesh,
        in_specs=placed,
        out_specs=P(("dp", "expert"), None),
        check_vma=False,
    )


def solution(mesh):
    return build(mesh, 4, 8)
```

time: 717 us -> 293 us (0.41)
  Pallas kernels: 0 us -> 288 us
  waiting for transfers between devices: 269 us -> 0 us
  blocking collectives: 240 us -> 0 us
  local copies, waits for them, and re-layouts: 98.5 us -> 2.3 us
  matrix products: 34.9 us -> 0 us
  other arithmetic: 33.9 us -> 0 us
  starting transfers between devices: 32.4 us -> 0 us
    pallas_call x0 -> x1, Pallas kernels: none -> 288 us  [shards(): pl.pallas_call(functools.partial(body, ny, nz, nx, (tok, width, rows, nch...]
    all_to_all x4 -> x0, waiting for transfers between devices: 269 us -> none  [the longest x1 94.9 us: shards(): lax.all_to_all(pair_tangent.reshape(owners, capacity, model_width), 'expe...]
    psum x1 -> x0, blocking collectives: 137 us -> none  [shards(): global_sum = lax.psum(local_sum, ('dp', 'expert'))]
    all_to_all x1 -> x0, blocking collectives: 102 us -> none  [shards(): lax.all_to_all(cotangent, 'expert', split_axis=0, concat_axis=0, tiled=True)]
    gather x6 -> x0, local copies, waits for them, and re-layouts: 44.5 us -> none  [the longest x2 14.1 us: shards(): jnp.take(jv_vals, source_token, axis=0) * source_gate[:, None]]
    reshape x10 -> x0, local copies, waits for them, and re-layouts: 41.9 us -> none  [the longest x1 4.69 us: shards(): x_rows = arrived[0].reshape(slot_total, model_width)]
    dot_general x7 -> x0, matrix products: 34.9 us -> none  [the longest x1 10.2 us: shards(): jnp.dot(hidden_tangent, down_w, preferred_element_type=jnp.float32)]
    all_to_all x4 -> x0, starting transfers between devices: 32.4 us -> none  [the longest x1 13.3 us: shards(): lax.all_to_all(send_x, 'expert', split_axis=0, concat_axis=0, tiled=True)]
  transfers between devices with their start and end apart: 4 -> 0, of which waited for: 3 -> 0; matrix products, arithmetic and copies ran while one was open for 3% -> 0% of each run, Pallas kernels for 0% -> 0%
where the time goes in v1:
time: 293 us; the launch traced here: 290 us
  Pallas kernels  288 us (98%)
    pallas_call x1, Pallas kernels, shards(): pl.pallas_call(functools.partial(body, ny, nz, nx, (tok, width, rows, nch...  288 us

profile of v1, /device:TPU:1, one launch (start us, length us, event | category | flops | bytes accessed | tf_op | source)
XLA Modules:
  0.0 289.9 jit_solution(4198587307383964537)
XLA Ops:
  0.0 287.6 %gauss_newton_moe.1 = f32[128,2048]{1,0:T(8,128)} custom-call(bf16[128,2048]{1,0:T(8,128)(2,1)} %x_hbm.1, bf16[128,2048]{1,0:T(8,128)(2,1)} %v_hbm.1, s32[4,128]{1,0:T(4,128)} %bitcast.2, f32[4,128]{1,0:T(4,128)} %bitcast.3, bf16[1,2048,768]{2,1,0:T(8,128)(2,1)} %wg_hbm.1, bf16[1,2048,768]{2,1,0:T(8,128)(2,1)} %wu_hbm.1, bf16[1,768,2048]{2,1,0:T(8,128)(2,1)} %wd_hbm.1), custom_call_target="tpu_custom_call" | custom-call | tf_op jit(solution)/shard_map/gauss_newton_moe/pallas_call | solution.py:497
  287.6 2.3 copy.9

commit v2 on v1

--- a/solution.py
+++ b/solution.py
@@ -11,6 +11,11 @@
 BF16 = jnp.bfloat16
 CAP = 9
 STG = 3
+HA = 1
+HB = 1
+HD = 1
+YL = 2
+NS = 2
 
 
 def body(
@@ -22,6 +27,7 @@
     tok, width, rows, nch, ff = dims
     peers = 2 * ny
     half = nz // 2
+    nitem = 2 * nch
     total = peers * rows
     me = lax.axis_index("expert")
     mx = lax.axis_index("dp")
@@ -54,14 +60,8 @@
     def load(i, hbm, ch):
         return local(hbm.at[:, pl.ds(ch * width, width)], g.at[i, mz], load_sem.at[i])
 
-    for ch in range(nch):
-        load(2 * ch, x_hbm, ch).start()
-        load(2 * ch + 1, v_hbm, ch).start()
-    for ch in range(nch):
-        local(wg_hbm.at[0, pl.ds(ch * width, width), :], wg.at[ch], w_sem.at[0]).start()
-        local(wu_hbm.at[0, pl.ds(ch * width, width), :], wu.at[ch], w_sem.at[1]).start()
-    for ch in range(nch):
-        local(wd_hbm.at[0, :, pl.ds(ch * width, width)], wd.at[ch], w_sem.at[2]).start()
+    for ch in range(min(2, nch)):
+        load(ch, x_hbm, ch).start()
 
     barrier = pltpu.get_barrier_semaphore()
     for k in range(1, nz):
@@ -74,6 +74,63 @@
         pl.semaphore_signal(
             barrier, inc=1, device_id={"dp": lax.rem(mx + k, nx)}, device_id_type=MESH
         )
+
+    pl.semaphore_wait(barrier, (nz - 1) + (peers - 1) + (nx - 1))
+
+    part_rows = tok // NS
+
+    def part(h):
+        return pl.ds(h * part_rows, part_rows)
+
+    def ag_send(i, slot, h, zs, dev):
+        piece = g.at[i, zs, part(h)]
+        remote(piece, piece, ag_s.at[i], ag_r.at[i, slot, h], dev).start()
+
+    def ag_wait(i, slot, h):
+        piece = g.at[i, mz, part(h)]
+        remote(piece, piece, ag_s.at[i], ag_r.at[i, slot, h], right).wait_recv()
+
+    def ag_first(i, h):
+        ag_send(i, 0, h, mz, right)
+        ag_send(i, 1, h, mz, left)
+
+    def ag_mid(i, s, h):
+        ag_wait(i, 2 * (s - 2), h)
+        ag_send(i, 2 * (s - 1), h, zoff(-(s - 1)), right)
+        ag_wait(i, 2 * (s - 2) + 1, h)
+        ag_send(i, 2 * (s - 1) + 1, h, zoff(s - 1), left)
+
+    def ag_far(i, h):
+        par = lax.rem(i, 2)
+        ag_wait(i, 2 * (half - 2), h)
+        ag_wait(i, 2 * (half - 2) + 1, h)
+        zs = jnp.where(par == 0, zoff(-(half - 1)), zoff(half - 1))
+        ag_send(i, 2 * half - 2, h, zs, jnp.where(par == 0, right, left))
+
+    def ag_done(i):
+        for h in range(NS):
+            ag_wait(i, 2 * half - 2, h)
+
+    def ag_drain(i):
+        local(g.at[i, pl.ds(0, nz - 1)], g.at[i, pl.ds(0, nz - 1)], ag_s.at[i]).wait()
+
+    def first(i, h):
+        if h == 0:
+            load(i, x_hbm, 0).wait()
+        ag_first(i, h)
+
+    for h in range(NS):
+        first(0, h)
+
+    for ch in range(2, nch):
+        load(ch, x_hbm, ch).start()
+    for ch in range(nch):
+        load(nch + ch, v_hbm, ch).start()
+    for ch in range(nch):
+        local(wg_hbm.at[0, pl.ds(ch * width, width), :], wg.at[ch], w_sem.at[0]).start()
+        local(wu_hbm.at[0, pl.ds(ch * width, width), :], wu.at[ch], w_sem.at[1]).start()
+    for ch in range(nch):
+        local(wd_hbm.at[0, :, pl.ds(ch * width, width)], wd.at[ch], w_sem.at[2]).start()
 
     pshift = peers.bit_length() - 1
     row = lax.broadcasted_iota(jnp.int32, (nz * peers, tok), 0)
@@ -105,39 +162,9 @@
             acc[m, pl.ds(pl.multiple_of(q * 16, 16), 16), :] = jnp.zeros((16, ff), F32)
 
     ssacc[...] = jnp.zeros(ssacc.shape, F32)
-    pl.semaphore_wait(barrier, (nz - 1) + (peers - 1) + (nx - 1))
-
     for k in range(1, nz):
         zt = zoff(k)
         remote(metas.at[zt], metar.at[mz], meta_sem.at[0], meta_sem.at[1], zdev(zt)).start()
-
-    def ag_send(i, slot, zs, dev):
-        remote(g.at[i, zs], g.at[i, zs], ag_s.at[i], ag_r.at[i, slot], dev).start()
-
-    def ag_wait(i, slot):
-        remote(g.at[i, mz], g.at[i, mz], ag_s.at[i], ag_r.at[i, slot], right).wait_recv()
-
-    def ag_first(i):
-        ag_send(i, 0, mz, right)
-        ag_send(i, 1, mz, left)
-
-    def ag_mid(i, s):
-        ag_wait(i, 2 * (s - 2))
-        ag_send(i, 2 * (s - 1), zoff(-(s - 1)), right)
-        ag_wait(i, 2 * (s - 2) + 1)
-        ag_send(i, 2 * (s - 1) + 1, zoff(s - 1), left)
-
-    def ag_far(i, par):
-        ag_wait(i, 2 * (half - 2))
-        ag_wait(i, 2 * (half - 2) + 1)
-        zs = jnp.where(par == 0, zoff(-(half - 1)), zoff(half - 1))
-        ag_send(i, 2 * half - 2, zs, jnp.where(par == 0, right, left))
-
-    def ag_done(i):
-        ag_wait(i, 2 * half - 2)
-
-    def ag_drain(i):
-        local(g.at[i, pl.ds(0, nz - 1)], g.at[i, pl.ds(0, nz - 1)], ag_s.at[i]).wait()
 
     def dispatch(i, slot):
         tokens = g[i].reshape(nz * tok, width)
@@ -177,38 +204,47 @@
 
     far = 2 * (half - 1)
 
-    def rs_send(j, src, slot, dev):
-        remote(src, rs.at[j, slot], rs_s.at[j], rs_r.at[j, slot], dev).start()
-
-    def rs_wait(j, slot):
-        remote(rs.at[j, slot], rs.at[j, slot], rs_s.at[j], rs_r.at[j, slot], right).wait_recv()
-
-    def rs_add(j, slot, zd):
-        rs[j, slot] = (rs[j, slot].astype(F32) + yb[j, zd].astype(F32)).astype(BF16)
-
-    def rs_first(j, par):
-        rs_send(j, yb.at[j, zoff(half)], far, jnp.where(par == 0, right, left))
+    def rs_send(j, src, slot, h, dev):
+        remote(src, rs.at[j, slot, part(h)], rs_s.at[j], rs_r.at[j, slot, h], dev).start()
+
+    def rs_wait(j, slot, h):
+        piece = rs.at[j, slot, part(h)]
+        remote(piece, piece, rs_s.at[j], rs_r.at[j, slot, h], right).wait_recv()
+
+    def rs_add(j, slot, h, zd):
+        rs[j, slot, part(h)] = (
+            rs[j, slot, part(h)].astype(F32) + yb[j, zd, part(h)].astype(F32)
+        ).astype(BF16)
+
+    def rs_first(j):
+        par = lax.rem(j, 2)
         zd = jnp.where(par == 0, zoff(-(half - 1)), zoff(half - 1))
-        rs_send(j, yb.at[j, zd], 1 - par, jnp.where(par == 0, left, right))
-
-    def rs_second(j, par):
-        rs_wait(j, far)
-        rs_add(j, far, jnp.where(par == 0, zoff(half - 1), zoff(-(half - 1))))
-        rs_send(j, rs.at[j, far], par, jnp.where(par == 0, right, left))
-
-    def rs_mid(j, s):
-        rs_wait(j, 2 * (s - 2))
-        rs_add(j, 2 * (s - 2), zoff(half - s))
-        rs_wait(j, 2 * (s - 2) + 1)
-        rs_add(j, 2 * (s - 2) + 1, zoff(-(half - s)))
-        rs_send(j, rs.at[j, 2 * (s - 2)], 2 * (s - 1), right)
-        rs_send(j, rs.at[j, 2 * (s - 2) + 1], 2 * (s - 1) + 1, left)
-
-    def rs_final(j):
-        rs_wait(j, far - 2)
-        rs_wait(j, far - 1)
+        for h in range(NS):
+            rs_send(j, yb.at[j, zoff(half), part(h)], far, h, jnp.where(par == 0, right, left))
+            rs_send(j, yb.at[j, zd, part(h)], 1 - par, h, jnp.where(par == 0, left, right))
+
+    def rs_second(j, h):
+        par = lax.rem(j, 2)
+        rs_wait(j, far, h)
+        rs_add(j, far, h, jnp.where(par == 0, zoff(half - 1), zoff(-(half - 1))))
+        rs_send(j, rs.at[j, far, part(h)], par, h, jnp.where(par == 0, right, left))
+
+    def rs_mid(j, s, h):
+        up = 2 * (s - 2)
+        rs_wait(j, up, h)
+        rs_add(j, up, h, zoff(half - s))
+        rs_send(j, rs.at[j, up, part(h)], up + 2, h, right)
+        rs_wait(j, up + 1, h)
+        rs_add(j, up + 1, h, zoff(-(half - s)))
+        rs_send(j, rs.at[j, up + 1, part(h)], up + 3, h, left)
+
+    def rs_final(j, h):
+        rs_wait(j, far - 2, h)
+        rs_wait(j, far - 1, h)
         return (
-            rs[j, far - 2].astype(F32) + rs[j, far - 1].astype(F32) + yb[j, mz].astype(F32)
+            rs[j, far - 2, part(h)].astype(F32)
+            + rs[j, far - 1, part(h)].astype(F32)
+            + yb[j, mz, part(h)].astype(F32)
         )
 
     def rs_drain(j):
@@ -221,21 +257,23 @@
         def _():
             fn(i)
 
-    nitem = 2 * nch
-
-    def first(i):
-        load(i, x_hbm, 0).wait()
-        ag_first(i)
-
     def products(i):
         dispatch_wait(i, lax.rem(i, STG))
-        ch = i // 2
-        m = lax.rem(i, 2) * 2
+        ch = lax.rem(i, nch)
+        m = (i // nch) * 2
         got = r[i].reshape(total, width)
         for n in range(ff // width):
             cols = slice(n * width, (n + 1) * width)
             acc[m, :, cols] += jnp.dot(got, wg[ch, :, cols], preferred_element_type=F32)
             acc[m + 1, :, cols] += jnp.dot(got, wu[ch, :, cols], preferred_element_type=F32)
+
+    def activate(q):
+        for k in range(rows // 16):
+            at_rows = pl.ds(pl.multiple_of(q * rows + k * 16, 16), 16)
+            a = acc[0, at_rows, :]
+            s = jax.nn.sigmoid(a)
+            acc[0, at_rows, :] = a * s
+            acc[1, at_rows, :] = s * (1.0 + a * (1.0 - s)) * acc[1, at_rows, :]
 
     def spread(i):
         ag_done(i)
@@ -264,27 +302,29 @@
         local(gsend.at[mp], grecv.at[mp], gate_sem.at[1]).start()
 
     def tick_a(t, carry):
-        at(half - 1, nitem, t, lambda i: ag_far(i, lax.rem(i, 2)))
-        for s in range(half - 1, 1, -1):
-            at(s - 1, nitem, t, lambda i, s=s: ag_mid(i, s))
-        at(0, nitem, t, first)
-
-        @pl.when(t == half - 1)
-        def _():
-            build()
-
-        at(half, nitem, t, spread)
-
-        @pl.when(t == half + 1)
+        for h in range(NS):
+            at(HA * (half - 1), nitem, t, lambda i, h=h: ag_far(i, h))
+            for s in range(half - 1, 1, -1):
+                at(HA * (s - 1), nitem, t, lambda i, s=s, h=h: ag_mid(i, s, h))
+            at(-1, nitem, t, lambda i, h=h: first(i, h))
+            if h == 0:
+                @pl.when(t == HA * half - 1)
+                def _():
+                    build()
+
+                at(HA * half, nitem, t, spread)
+
+        @pl.when(t == HA * half + 1)
         def _():
             for q, (hbm, vm) in enumerate(((wg_hbm, wg), (wu_hbm, wu), (wd_hbm, wd))):
                 local(vm, vm, w_sem.at[q]).wait()
 
-        at(half + 2, nitem, t, products)
-        at(half + 2, nitem, t, ag_drain)
+        at(HA * half + YL, nitem, t, products)
+        at(nch + HA * half + YL, peers, t, activate)
+        at(HA * half + YL, nitem, t, ag_drain)
         return carry
 
-    lax.fori_loop(0, nitem + half + 2, tick_a, 0)
+    lax.fori_loop(0, nitem + HA * half + YL, tick_a, 0)
 
     local(grecv, grecv, gate_sem.at[1]).wait()
     local(gsend.at[pl.ds(0, peers - 1)], gsend.at[pl.ds(0, peers - 1)], gate_sem.at[0]).wait()
@@ -292,14 +332,9 @@
     @pl.loop(0, total // 16)
     def _(q):
         at_rows = pl.ds(pl.multiple_of(q * 16, 16), 16)
-        a = acc[0, at_rows, :]
-        b = acc[1, at_rows, :]
-        s = jax.nn.sigmoid(a)
-        act = a * s
-        slope_b = s * (1.0 + a * (1.0 - s)) * b
-        hid[at_rows, :] = (slope_b * acc[2, at_rows, :] + act * acc[3, at_rows, :]).astype(BF16)
-        acc[0, at_rows, :] = act
-        acc[1, at_rows, :] = slope_b
+        hid[at_rows, :] = (
+            acc[1, at_rows, :] * acc[2, at_rows, :] + acc[0, at_rows, :] * acc[3, at_rows, :]
+        ).astype(BF16)
         acc[2, at_rows, :] = jnp.zeros((16, ff), F32)
 
     def gate_lanes():
@@ -314,51 +349,53 @@
 
     def home(j):
         combine(j, lax.rem(j, STG))
-        rs_first(j, lax.rem(j, 2))
-
-    def finish_jv(j):
-        jv = rs_final(j) + g[2 * j + 1, mz].astype(F32)
-        jvf[j] = jv
-        ssacc[...] += jv * jv
-        g[2 * j, mz] = jv.astype(BF16)
-        ag_first(2 * j)
+        rs_first(j)
+
+    def finish_jv(j, h):
+        jv = rs_final(j, h) + g[nch + j, mz, part(h)].astype(F32)
+        jvf[j, part(h)] = jv
+        ssacc[part(h)] += jv * jv
+        g[j, mz, part(h)] = jv.astype(BF16)
+        ag_first(j, h)
 
     def spread_jv(j):
         rs_drain(j)
-        ag_done(2 * j)
-        dispatch(2 * j, lax.rem(j, STG))
-        dispatch_send(2 * j, lax.rem(j, STG))
+        ag_done(j)
+        dispatch(j, lax.rem(j, STG))
+        dispatch_send(j, lax.rem(j, STG))
 
     contract_last = (((1,), (1,)), ((), ()))
 
     def back(j):
-        dispatch_wait(2 * j, lax.rem(j, STG))
-        ag_drain(2 * j)
-        got = r[2 * j].reshape(total, width)
+        dispatch_wait(j, lax.rem(j, STG))
+        ag_drain(j)
+        got = r[j].reshape(total, width)
         for n in range(ff // width):
             cols = slice(n * width, (n + 1) * width)
             acc[2, :, cols] += lax.dot_general(
                 got, wd[j, cols, :], contract_last, preferred_element_type=F32
             )
 
-    rl = 2
-    al = rl + half
+    rl = YL
+    al = rl + HB * half
 
     def tick_b(t, carry):
-        at(al + half - 1, nch, t, lambda j: ag_far(2 * j, lax.rem(j, 2)))
-        for s in range(half - 1, 1, -1):
-            at(al + s - 1, nch, t, lambda j, s=s: ag_mid(2 * j, s))
-        for s in range(half - 1, 1, -1):
-            at(rl + s, nch, t, lambda j, s=s: rs_mid(j, s))
-        at(rl + 1, nch, t, lambda j: rs_second(j, lax.rem(j, 2)))
-        at(al, nch, t, finish_jv)
-        at(0, nch, t, tangent_out)
-        at(al + half, nch, t, spread_jv)
+        for h in range(NS):
+            at(al + HB * (half - 1), nch, t, lambda j, h=h: ag_far(j, h))
+            for s in range(half - 1, 1, -1):
+                at(al + HB * (s - 1), nch, t, lambda j, s=s, h=h: ag_mid(j, s, h))
+            for s in range(half - 1, 1, -1):
+                at(rl + HB * s, nch, t, lambda j, s=s, h=h: rs_mid(j, s, h))
+            at(rl + HB, nch, t, lambda j, h=h: rs_second(j, h))
+            at(al, nch, t, lambda j, h=h: finish_jv(j, h))
+            if h == 0:
+                at(al + HB * half, nch, t, spread_jv)
+                at(0, nch, t, tangent_out)
         at(rl, nch, t, home)
-        at(al + half + 2, nch, t, back)
+        at(al + HB * half + YL, nch, t, back)
         return carry
 
-    lax.fori_loop(0, nch + al + half + 2, tick_b, 0)
+    lax.fori_loop(0, nch + al + HB * half + YL, tick_b, 0)
 
     def exchange(stage, me_slot, count, dev_of):
         for k in range(1, count):
@@ -378,8 +415,8 @@
             value = value + red[stage, k]
         return value
 
-    part = jnp.sum(jnp.sum(ssacc[...], axis=1, keepdims=True), axis=0, keepdims=True)
-    red[0, mp] = jnp.broadcast_to(part, (8, 128))
+    squares = jnp.sum(jnp.sum(ssacc[...], axis=1, keepdims=True), axis=0, keepdims=True)
+    red[0, mp] = jnp.broadcast_to(squares, (8, 128))
     if peers > 1:
         exchange(0, mp, peers, lambda d: {"expert": pdev(d)})
 
@@ -391,9 +428,6 @@
         gru[0, at_rows, :] = (bk * acc[1, at_rows, :]).astype(BF16)
         gru[1, at_rows, :] = (bk * acc[0, at_rows, :]).astype(BF16)
 
-    red[1, mz] = gathered(0, peers)
-    exchange(1, mz, nz, lambda d: {"expert": zdev(d)})
-
     def grad_out(j):
         slot = lax.rem(j, STG)
         pg = lax.dot_general(gru[0], wg[j], contract_last, preferred_element_type=F32)
@@ -404,23 +438,34 @@
     def out_copy(j, slot):
         return local(ostg.at[slot], out_hbm.at[:, pl.ds(pl.multiple_of(j * width, width), width)], o_sem.at[slot])
 
-    def finish_out(j):
+    def finish_out(j, h):
         slot = lax.rem(j, 2)
-
-        @pl.when(j >= 2)
+        if h == 0:
+            @pl.when(j >= 2)
+            def _():
+                out_copy(j - 2, slot).wait()
+
+        mean = red[3, 0][0:1, 0:1] * (1.0 / (tok * nx * ny * nz * 2.0 * nch * width))
+        scale = jnp.broadcast_to(lax.rsqrt(mean + 1e-06), (part_rows, width))
+        ostg[slot, part(h)] = (rs_final(j, h) + jvf[j, part(h)]) * scale
+        if h == NS - 1:
+            out_copy(j, slot).start()
+
+    dl = rl + HD * half
+
+    def tick_d(t, carry):
+        for h in range(NS):
+            for s in range(half - 1, 1, -1):
+                at(rl + HD * s, nch, t, lambda j, s=s, h=h: rs_mid(j, s, h))
+            at(rl + HD, nch, t, lambda j, h=h: rs_second(j, h))
+            if h == 0:
+                at(0, nch, t, grad_out)
+
+        @pl.when(t == 1)
         def _():
-            out_copy(j - 2, slot).wait()
-
-        mean = red[3, 0][0:1, 0:1] * (1.0 / (tok * nx * ny * nz * 2.0 * nch * width))
-        scale = jnp.broadcast_to(lax.rsqrt(mean + 1e-06), (tok, width))
-        ostg[slot] = (rs_final(j) + jvf[j]) * scale
-        out_copy(j, slot).start()
-
-    def tick_d(t, carry):
-        for s in range(half - 1, 1, -1):
-            at(rl + s, nch, t, lambda j, s=s: rs_mid(j, s))
-        at(rl + 1, nch, t, lambda j: rs_second(j, lax.rem(j, 2)))
-        at(0, nch, t, grad_out)
+            red[1, mz] = gathered(0, peers)
+            exchange(1, mz, nz, lambda d: {"expert": zdev(d)})
+
         at(rl, nch, t, home)
 
         @pl.when(t == rl + 1)
@@ -429,14 +474,15 @@
             if nx > 1:
                 exchange(2, mx, nx, lambda d: {"dp": d})
 
-        @pl.when(t == al)
+        @pl.when(t == dl)
         def _():
             red[3, 0] = gathered(2, nx) if nx > 1 else red[2, 0]
 
-        at(al, nch, t, finish_out)
+        for h in range(NS):
+            at(dl, nch, t, lambda j, h=h: finish_out(j, h))
         return carry
 
-    lax.fori_loop(0, nch + al, tick_d, 0)
+    lax.fori_loop(0, nch + dl, tick_d, 0)
     for j in range(nch):
         rs_drain(j)
     for j in range(max(0, nch - 2), nch):
@@ -479,13 +525,13 @@
         pltpu.VMEM((tok, width), F32),
         dma((2 * nch,)),
         dma((3,)),
-        dma((2 * nch, nz - 1)),
+        dma((2 * nch, nz - 1, NS)),
         dma((2 * nch,)),
         dma((2 * nch,)),
         dma((STG,)),
         dma((nch,)),
         dma((STG,)),
-        dma((nch, nz - 1)),
+        dma((nch, nz - 1, NS)),
         dma((nch,)),
         dma((2,)),
         dma((2,)),

time: 293 us -> 279 us (0.952)
  Pallas kernels: 288 us -> 272 us
    pallas_call x1, Pallas kernels: 288 us -> 272 us  [shards(): pl.pallas_call(functools.partial(body, ny, nz, nx, (tok, width, rows, nch...]
where the time goes in v2:
time: 279 us; the launch traced here: 274 us
  Pallas kernels  272 us (97%)
    pallas_call x1, Pallas kernels, shards(): pl.pallas_call(functools.partial(body, ny, nz, nx, (tok, width, rows, nch...  272 us

profile of v2, /device:TPU:1, one launch (start us, length us, event | category | flops | bytes accessed | tf_op | source)
XLA Modules:
  0.0 274.4 jit_solution(10210561736593855525)
XLA Ops:
  0.0 272.1 %gauss_newton_moe.1 = f32[128,2048]{1,0:T(8,128)} custom-call(bf16[128,2048]{1,0:T(8,128)(2,1)} %x_hbm.1, bf16[128,2048]{1,0:T(8,128)(2,1)} %v_hbm.1, s32[4,128]{1,0:T(4,128)} %bitcast.2, f32[4,128]{1,0:T(4,128)} %bitcast.3, bf16[1,2048,768]{2,1,0:T(8,128)(2,1)} %wg_hbm.1, bf16[1,2048,768]{2,1,0:T(8,128)(2,1)} %wu_hbm.1, bf16[1,768,2048]{2,1,0:T(8,128)(2,1)} %wd_hbm.1), custom_call_target="tpu_custom_call" | custom-call | tf_op jit(solution)/shard_map/gauss_newton_moe/pallas_call | solution.py:543
  272.1 2.3 copy.9

commit v3 on v2

--- a/solution.py
+++ b/solution.py
@@ -168,10 +168,8 @@
 
     def dispatch(i, slot):
         tokens = g[i].reshape(nz * tok, width)
-        for d in range(peers):
-            stg[slot, d] = jnp.dot(
-                sel[d * rows : (d + 1) * rows, :], tokens, preferred_element_type=F32
-            ).astype(BF16)
+        picked = jnp.dot(sel[...], tokens, preferred_element_type=F32)
+        stg[slot] = picked.astype(BF16).reshape(peers, rows, width)
 
     def dispatch_send(i, slot):
         for k in range(1, peers):
@@ -197,10 +195,8 @@
             rstg.at[slot, pl.ds(0, peers - 1)], rstg.at[slot, pl.ds(0, peers - 1)], rt_s.at[slot]
         ).wait()
         back_rows = ret[j].reshape(total, width)
-        for zs in range(nz):
-            yb[j, zs] = jnp.dot(
-                selt[zs * tok : (zs + 1) * tok, :], back_rows, preferred_element_type=F32
-            ).astype(BF16)
+        sums = jnp.dot(selt[...], back_rows, preferred_element_type=F32)
+        yb[j] = sums.astype(BF16).reshape(nz, tok, width)
 
     far = 2 * (half - 1)
 
@@ -390,8 +386,8 @@
             at(al, nch, t, lambda j, h=h: finish_jv(j, h))
             if h == 0:
                 at(al + HB * half, nch, t, spread_jv)
-                at(0, nch, t, tangent_out)
-        at(rl, nch, t, home)
+                at(rl, nch, t, home)
+        at(0, nch, t, tangent_out)
         at(al + HB * half + YL, nch, t, back)
         return carry
 
@@ -459,14 +455,13 @@
                 at(rl + HD * s, nch, t, lambda j, s=s, h=h: rs_mid(j, s, h))
             at(rl + HD, nch, t, lambda j, h=h: rs_second(j, h))
             if h == 0:
-                at(0, nch, t, grad_out)
+                at(rl, nch, t, home)
+        at(0, nch, t, grad_out)
 
         @pl.when(t == 1)
         def _():
             red[1, mz] = gathered(0, peers)
             exchange(1, mz, nz, lambda d: {"expert": zdev(d)})
-
-        at(rl, nch, t, home)
 
         @pl.when(t == rl + 1)
         def _():

time: 279 us -> 271 us (0.971)
  Pallas kernels: 272 us -> 266 us
    pallas_call x1, Pallas kernels: 272 us -> 266 us  [shards(): pl.pallas_call(functools.partial(body, ny, nz, nx, (tok, width, rows, nch...]
where the time goes in v3:
time: 271 us; the launch traced here: 269 us
  Pallas kernels  266 us (98%)
    pallas_call x1, Pallas kernels, shards(): pl.pallas_call(functools.partial(body, ny, nz, nx, (tok, width, rows, nch...  266 us

profile of v3, /device:TPU:1, one launch (start us, length us, event | category | flops | bytes accessed | tf_op | source)
XLA Modules:
  0.0 268.8 jit_solution(12384685875122697315)
XLA Ops:
  0.0 266.5 %gauss_newton_moe.1 = f32[128,2048]{1,0:T(8,128)} custom-call(bf16[128,2048]{1,0:T(8,128)(2,1)} %x_hbm.1, bf16[128,2048]{1,0:T(8,128)(2,1)} %v_hbm.1, s32[4,128]{1,0:T(4,128)} %bitcast.2, f32[4,128]{1,0:T(4,128)} %bitcast.3, bf16[1,2048,768]{2,1,0:T(8,128)(2,1)} %wg_hbm.1, bf16[1,2048,768]{2,1,0:T(8,128)(2,1)} %wu_hbm.1, bf16[1,768,2048]{2,1,0:T(8,128)(2,1)} %wd_hbm.1), custom_call_target="tpu_custom_call" | custom-call | tf_op jit(solution)/shard_map/gauss_newton_moe/pallas_call | solution.py:538
  266.5 2.3 copy.9

commit v4 on v3

--- a/solution.py
+++ b/solution.py
@@ -166,14 +166,19 @@
         zt = zoff(k)
         remote(metas.at[zt], metar.at[mz], meta_sem.at[0], meta_sem.at[1], zdev(zt)).start()
 
+    far_first = sorted(
+        [(dy, dc) for dy in range(ny) for dc in range(2) if (dy, dc) != (0, 0)],
+        key=lambda p: (-min(p[0], ny - p[0]), p[1], p[0]),
+    )
+
     def dispatch(i, slot):
         tokens = g[i].reshape(nz * tok, width)
         picked = jnp.dot(sel[...], tokens, preferred_element_type=F32)
         stg[slot] = picked.astype(BF16).reshape(peers, rows, width)
 
     def dispatch_send(i, slot):
-        for k in range(1, peers):
-            d = lax.rem(mp + k, peers)
+        for dy, dc in far_first:
+            d = lax.rem(my + dy, ny) * 2 + lax.rem(mc + dc, 2)
             remote(stg.at[slot, d], r.at[i, mp], y_s.at[slot], y_r.at[i], pdev(d)).start()
         local(stg.at[slot, mp], r.at[i, mp], y_r.at[i]).start()
 
@@ -184,8 +189,8 @@
         ).wait()
 
     def return_send(j, slot):
-        for k in range(1, peers):
-            d = lax.rem(mp + k, peers)
+        for dy, dc in far_first:
+            d = lax.rem(my + dy, ny) * 2 + lax.rem(mc + dc, 2)
             remote(rstg.at[slot, d], ret.at[j, mp], rt_s.at[slot], rt_r.at[j], pdev(d)).start()
         local(rstg.at[slot, mp], ret.at[j, mp], rt_r.at[j]).start()
 

time: 271 us -> 271 us (level)
  no operation moved by 1% of the time
where the time goes in v4:
time: 271 us; the launch traced here: 269 us
  Pallas kernels  266 us (98%)
    pallas_call x1, Pallas kernels, shards(): pl.pallas_call(functools.partial(body, ny, nz, nx, (tok, width, rows, nch...  266 us

profile of v4, /device:TPU:1, one launch (start us, length us, event | category | flops | bytes accessed | tf_op | source)
XLA Modules:
  0.0 268.7 jit_solution(16305755906272826592)
XLA Ops:
  0.0 266.4 %gauss_newton_moe.1 = f32[128,2048]{1,0:T(8,128)} custom-call(bf16[128,2048]{1,0:T(8,128)(2,1)} %x_hbm.1, bf16[128,2048]{1,0:T(8,128)(2,1)} %v_hbm.1, s32[4,128]{1,0:T(4,128)} %bitcast.2, f32[4,128]{1,0:T(4,128)} %bitcast.3, bf16[1,2048,768]{2,1,0:T(8,128)(2,1)} %wg_hbm.1, bf16[1,2048,768]{2,1,0:T(8,128)(2,1)} %wu_hbm.1, bf16[1,768,2048]{2,1,0:T(8,128)(2,1)} %wd_hbm.1), custom_call_target="tpu_custom_call" | custom-call | tf_op jit(solution)/shard_map/gauss_newton_moe/pallas_call | solution.py:543
  266.4 2.3 copy.9
